TPU v7x, 256 devices: a whole 4x4x8 slice. The times are simulated.
256 devices in a mesh: section: 2 (over y_hi), seq: 32 (over x, z), chan: 4 (over y_lo, core).
Axes of the slice: x: 4, y: 4 (y_hi: 2, y_lo: 2; y = y_hi * 2 + y_lo), z: 8, core: 2. Of those that a mesh axis runs over, the one named last changes fastest.
Arguments:
- bases: int32 [2, 2097152], P('section', 'seq'), may hold values from 0 to 3
- stem_embedding_weight: bfloat16 [512, 1536], P(None, 'chan'), may hold values from -1.64443437 to 1.64443437
- gains: float32 [3, 1536], replicated, may hold values from 0.1 to 1.9
- conv_weight: bfloat16 [3, 3, 1536, 1536], P(None, None, None, 'chan'), may hold values from -0.09375 to 0.09375
- dec_weight: bfloat16 [1536, 384], P('chan'), may hold values from -0.3125 to 0.3125
- upstream: bfloat16 [2, 16384, 1536], P('section', 'seq', 'chan'), may hold values from -0.032958984 to 0.032958984
Outputs:
- decoded: bfloat16 [2, 16384, 1536], P('section', 'seq', 'chan')
- weight_grad: float32 [1536, 384], P('chan')
All inputs are finite; a program needn't handle non-finite values.
Results may differ from a plain program's by a relative error of at most 0.0076.
Values may be sent and summed in bfloat16 or wider, within the bound.
No kernel may reach another device: no remote copies, remote signals or barrier semaphores. Data moves between devices by JAX's collectives and lax.ppermute only.
A program may use at most 128 MiB of HBM per device.

v0:
```python
import jax
import jax.numpy as jnp
from jax import lax
from jax.sharding import PartitionSpec as P

PATCH = 128
FIRST_DILATION0 = 2
EPSILON = 1e-06


def with_halo(shard, sides, width):
    for axis, dim in sides:
        size, length = (lax.axis_size(axis), shard.shape[dim])
        up = [(i, (i + 1) % size) for i in range(size - 1)]
        down = [(j, i) for i, j in up]
        last = lax.slice_in_dim(shard, length - width, length, axis=dim)
        initial = lax.slice_in_dim(shard, 0, width, axis=dim)
        before = lax.ppermute(last, axis, up)
        after = lax.ppermute(initial, axis, down)
        shard = jnp.concatenate([before, shard, after], axis=dim)
    return shard


def activate(rows, gain_row):
    widened = rows.astype(jnp.float32)
    inverse_rms = lax.rsqrt(jnp.mean(widened * widened, axis=-1, keepdims=True) + EPSILON)
    return jax.nn.gelu(widened * inverse_rms * gain_row).astype(jnp.bfloat16)


def apply_convolution(padded, kernel_taps, dilation_step, row_count):
    update = jnp.dot(padded[0:row_count], kernel_taps[0], preferred_element_type=jnp.float32)
    for offset in range(1, kernel_taps.shape[0]):
        start = offset * dilation_step
        update = update + jnp.dot(
            padded[start : start + row_count],
            kernel_taps[offset],
            preferred_element_type=jnp.float32,
        )
    return update


def body(bases, stem_embedding_weight, gains, conv_weight, dec_weight, upstream):
    row_count = upstream.shape[1]
    letters = bases.reshape(row_count, PATCH)
    onehot = letters[:, :, None] == jnp.arange(4, dtype=jnp.int32)[None, None, :]
    onehot = onehot.astype(jnp.bfloat16).reshape(row_count, PATCH * 4)
    stream = jnp.dot(onehot, stem_embedding_weight, preferred_element_type=jnp.float32).astype(
        jnp.bfloat16
    )
    for tower_layer_index in range(conv_weight.shape[0]):
        dilation_step = FIRST_DILATION0 * 2**tower_layer_index
        full_rows = lax.all_gather(stream, "chan", axis=1, tiled=True)
        padded = with_halo(
            activate(full_rows, gains[tower_layer_index]), (("seq", 0),), dilation_step
        )
        update = apply_convolution(padded, conv_weight[tower_layer_index], dilation_step, row_count)
        stream = (stream.astype(jnp.float32) + update).astype(jnp.bfloat16)
    decoded = jnp.dot(stream, dec_weight, preferred_element_type=jnp.float32).astype(jnp.bfloat16)
    upstream_rows = upstream[0]
    contract_row_pairs = (((0,), (0,)), ((), ()))
    partial_grad = lax.dot_general(
        stream, upstream_rows, contract_row_pairs, preferred_element_type=jnp.float32
    )
    weight_grad = lax.psum(partial_grad, ("section", "seq"))
    return (decoded[None], weight_grad)


def solution(mesh):
    placed = (
        P("section", "seq"),
        P(None, "chan"),
        P(),
        P(None, None, None, "chan"),
        P("chan", None),
        P("section", "seq", "chan"),
    )
    return jax.shard_map(
        body,
        mesh=mesh,
        in_specs=placed,
        out_specs=(P("section", "seq", "chan"), P("chan", None)),
        check_vma=False,
    )
```

profile of v0, /device:TPU:24, one launch (start us, length us, event | category | flops | bytes accessed | tf_op | source)
XLA Modules:
  0.0 813.8 jit_solution(4729358638135030658)
XLA Ops:
  10.5 29.4 %all-gather.4.cloned.1.call-done = bf16[512,1536]{1,0:T(8,128)(2,1)} async-done(((bf16[512,384]{1,0:T(8,128)(2,1)}), bf16[512,1536]{1,0:T(8,128)(2,1)}) %all-gather.4.cloned.1.call-update) | async-done | bytes 1572880 | tf_op jit(solution)/shard_map/all_gather | solution.py:52
  39.8 1.8 fusion
  41.6 2.8 fusion.4
  44.5 3.5 collective-permute-start
  49.2 2.2 fusion.60
  51.5 2.0 collective-permute-done.1
  53.4 2.3 fusion.38
  55.7 3.1 fusion.49
  58.8 28.8 %all-gather.6.cloned.1.call-done = bf16[512,1536]{1,0:T(8,128)(2,1)} async-done(((bf16[512,384]{1,0:T(8,128)(2,1)}), bf16[512,1536]{1,0:T(8,128)(2,1)}) %all-gather.6.cloned.1.call-update) | async-done | bytes 1572880 | tf_op jit(solution)/shard_map/all_gather | solution.py:52
  87.6 1.8 fusion.9
  89.4 2.8 fusion.13
  93.5 2.2 fusion.56
  95.8 4.7 collective-permute-start.2
  100.5 2.3 fusion.34
  102.8 3.0 add_convert_fusion.1
  105.9 29.4 %all-gather.8.cloned.1.call-done = bf16[512,1536]{1,0:T(8,128)(2,1)} async-done(((bf16[512,384]{1,0:T(8,128)(2,1)}), bf16[512,1536]{1,0:T(8,128)(2,1)}) %all-gather.8.cloned.1.call-update) | async-done | bytes 1572880 | tf_op jit(solution)/shard_map/all_gather | solution.py:52
  135.3 1.8 fusion.18
  137.1 2.8 fusion.22
  141.4 2.2 fusion.52
  143.7 4.7 collective-permute-start.4
  148.4 2.2 fusion.30
  150.7 2.3 add_convert_fusion
  155.4 649.9 %all-reduce.2.cloned.1.call-done = f32[384,384]{1,0:T(8,128)} async-done(((f32[384,384]{1,0:T(8,128)}), f32[384,384]{1,0:T(8,128)}) %all-reduce.2.cloned.1.call-update) | async-done | bytes 589840 | tf_op jit(solution)/shard_map/psum | solution.py:64
  805.3 1.9 copy.10
  (45 shorter events, 9.9 us)
Async XLA Ops:
  7.2 1.8 copy-start
  7.2 3.2 copy-start.6
  7.2 32.7 %all-gather.4.cloned.1.call-start = ((), (), s32[]{:S(2)}) async-start(), calls=%async_computation | async-start | bytes 1966080 | tf_op jit(solution)/shard_map/all_gather | solution.py:52
  10.4 77.3 %all-gather.6.cloned.1.call-start = ((), (), s32[]{:S(2)}) async-start(), calls=%async_computation.1 | async-start | bytes 1966080 | tf_op jit(solution)/shard_map/all_gather | solution.py:52
  44.5 11.2 %collective-permute-start = (bf16[2,1536]{1,0:T(2,128)(2,1)S(1)}, bf16[2,1536]{1,0:T(2,128)(2,1)S(1)}, u32[]{:S(2)}, u32[]{:S(2)}) collective-permute-start(bf16[2,1536]{1,0:T(2,128)(2,1)S(1)} %get-tuple-element.9), channel_id=1, source_target_pairs={{0,4},{4,8},{8,12},{12,16},{16,20},{20,24},{24,28},{28,32},{32,36}... | collective-permute-start | bytes 18440 | tf_op jit(solution)/shard_map/ppermute | solution.py:18
  47.9 5.5 collective-permute-start.1
  51.5 4.2 copy-start.1
  58.8 76.5 %all-gather.8.cloned.1.call-start = ((), (), s32[]{:S(2)}) async-start(), calls=%async_computation.2 | async-start | bytes 1966080 | tf_op jit(solution)/shard_map/all_gather | solution.py:52
  92.2 8.3 %collective-permute-start.3 = (bf16[4,1536]{1,0:T(4,128)(2,1)S(1)}, bf16[4,1536]{1,0:T(4,128)(2,1)S(1)}, u32[]{:S(2)}, u32[]{:S(2)}) collective-permute-start(bf16[4,1536]{1,0:T(4,128)(2,1)S(1)} %get-tuple-element.8), channel_id=1, source_target_pairs={{4,0},{8,4},{12,8},{16,12},{20,16},{24,20},{28,24},{32,28},{36,32}... | collective-permute-start | bytes 36872 | tf_op jit(solution)/shard_map/ppermute | solution.py:19
  95.8 7.0 copy-start.3
  95.8 7.0 collective-permute-start.2
  105.9 699.5 %all-reduce.2.cloned.1.call-start = ((), (), s32[]{:S(2)}) async-start(), calls=%async_computation.3 | async-start | bytes 1179648 | tf_op jit(solution)/shard_map/psum | solution.py:64
  139.9 8.4 %collective-permute-start.5 = (bf16[8,1536]{1,0:T(8,128)(2,1)S(1)}, bf16[8,1536]{1,0:T(8,128)(2,1)S(1)}, u32[]{:S(2)}, u32[]{:S(2)}) collective-permute-start(bf16[8,1536]{1,0:T(8,128)(2,1)S(1)} %get-tuple-element.6), channel_id=1, source_target_pairs={{4,0},{8,4},{12,8},{16,12},{20,16},{24,20},{28,24},{32,28},{36,32}... | collective-permute-start | bytes 73736 | tf_op jit(solution)/shard_map/ppermute | solution.py:19
  143.7 7.0 copy-start.2
  143.7 7.0 collective-permute-start.4
  150.6 2.4 copy-start.4
  150.6 3.6 copy-start.5
Sparse Core Ops, SparseCore 0:
  10.5 29.3 all-gather.3
  58.9 28.6 all-gather.5
  106.0 29.3 all-gather.7
  154.4 650.8 all-reduce.1
where the time goes:
time: 815 us; the launch traced here: 814 us
  waiting for transfers between devices  740 us (91%)
  matrix products  25.6 us (3%)
  starting transfers between devices  17 us (2%)
  between operations  14.1 us (2%)
  other arithmetic  13.7 us (2%)
    psum x1, waiting for transfers between devices, body(): weight_grad = lax.psum(partial_grad, ('section', 'seq'))  650 us
    all_gather x3, waiting for transfers between devices, body(): full_rows = lax.all_gather(stream, 'chan', axis=1, tiled=True)  87.6 us
  transfers between devices with their start and end apart: 10, of which 5 were waited for; matrix products, arithmetic and copies ran while one was open for 2% of the time, Pallas kernels for 0%

commit v1 on v0

--- a/solution.py
+++ b/solution.py
@@ -49,7 +49,9 @@
     )
     for tower_layer_index in range(conv_weight.shape[0]):
         dilation_step = FIRST_DILATION0 * 2**tower_layer_index
-        full_rows = lax.all_gather(stream, "chan", axis=1, tiled=True)
+        full_rows = jnp.concatenate(
+            lax.all_to_all(jnp.stack([stream] * lax.axis_size("chan")), "chan", 0, 0), axis=1
+        )
         padded = with_halo(
             activate(full_rows, gains[tower_layer_index]), (("seq", 0),), dilation_step
         )

time: 815 us -> 821 us (level)
  starting transfers between devices: 17 us -> 32.5 us
  waiting for transfers between devices: 740 us -> 729 us
    all_gather x3 -> x0, waiting for transfers between devices: 87.6 us -> none  [body(): full_rows = lax.all_gather(stream, 'chan', axis=1, tiled=True)]
    all_to_all x0 -> x3, waiting for transfers between devices: none -> 55.2 us  [body(): lax.all_to_all(jnp.stack([stream] * lax.axis_size('chan')), 'chan', 0, 0)]
    all_to_all x0 -> x3, starting transfers between devices: none -> 14.1 us  [body(): lax.all_to_all(jnp.stack([stream] * lax.axis_size('chan')), 'chan', 0, 0)]
    ppermute x3, waiting for transfers between devices: 1.97 us -> 14.5 us  [with_halo(): after = lax.ppermute(initial, axis, down)]
  transfers between devices with their start and end apart: 10 -> 10, of which waited for: 5 -> 9; matrix products, arithmetic and copies ran while one was open for 2% -> 3% of each run, Pallas kernels for 0% -> 0%
where the time goes in v1:
time: 821 us; the launch traced here: 820 us
  waiting for transfers between devices  729 us (89%)
  starting transfers between devices  32.5 us (4%)
  matrix products  26.8 us (3%)
  between operations  14.3 us (2%)
  other arithmetic  9.2 us (1%)
  local copies, waits for them, and re-layouts  8.8 us (1%)
    psum x1, waiting for transfers between devices, body(): weight_grad = lax.psum(partial_grad, ('section', 'seq'))  655 us
    all_to_all x3, waiting for transfers between devices, body(): lax.all_to_all(jnp.stack([stream] * lax.axis_size('chan')), 'chan', 0, 0)  55.2 us
  transfers between devices with their start and end apart: 10, of which 9 were waited for; matrix products, arithmetic and copies ran while one was open for 3% of the time, Pallas kernels for 0%

profile of v1, /device:TPU:24, one launch (start us, length us, event | category | flops | bytes accessed | tf_op | source)
XLA Modules:
  0.0 820.2 jit_solution(1852829571077277816)
XLA Ops:
  11.0 4.3 all-to-all-start
  15.4 18.3 %all-to-all-done = bf16[4,512,384]{1,2,0:T(8,128)(2,1)S(1)} async-done(((bf16[4,512,384]{1,2,0:T(8,128)(2,1)}), bf16[4,512,384]{1,2,0:T(8,128)(2,1)S(1)}, u32[]{:S(2)}, u32[]{:S(2)}) %all-to-all-start) | async-done | bytes 1572896 | tf_op jit(solution)/shard_map/all_to_all | solution.py:53
  35.7 3.8 collective-permute-start
  42.2 2.3 fusion.81
  44.4 7.8 collective-permute-done.1
  52.2 2.8 fusion.59
  55.1 2.8 fusion.70
  59.4 4.9 all-to-all-start.1
  64.3 18.4 %all-to-all-done.1 = bf16[4,512,384]{1,2,0:T(8,128)(2,1)S(1)} async-done(((bf16[4,512,384]{1,2,0:T(8,128)(2,1)}), bf16[4,512,384]{1,2,0:T(8,128)(2,1)S(1)}, u32[]{:S(2)}, u32[]{:S(2)}) %all-to-all-start.1) | async-done | bytes 1572896 | tf_op jit(solution)/shard_map/all_to_all | solution.py:53
  87.5 2.3 fusion.77
  89.8 4.6 collective-permute-start.2
  94.4 3.3 collective-permute-done.3
  97.7 2.8 fusion.55
  100.5 2.2 collective-permute-done.2
  102.7 2.8 add_convert_fusion.1
  107.0 4.9 all-to-all-start.2
  112.0 18.4 %all-to-all-done.2 = bf16[4,512,384]{1,2,0:T(8,128)(2,1)S(1)} async-done(((bf16[4,512,384]{1,2,0:T(8,128)(2,1)}), bf16[4,512,384]{1,2,0:T(8,128)(2,1)S(1)}, u32[]{:S(2)}, u32[]{:S(2)}) %all-to-all-start.2) | async-done | bytes 1572896 | tf_op jit(solution)/shard_map/all_to_all | solution.py:53
  134.9 2.3 fusion.73
  137.2 5.9 collective-permute-start.4
  143.1 3.4 collective-permute-done.5
  146.5 2.8 fusion.51
  149.4 2.0 collective-permute-done.4
  151.3 2.8 add_convert_fusion
  156.6 654.8 %all-reduce.2.cloned.1.call-done = f32[384,384]{1,0:T(8,128)} async-done(((f32[384,384]{1,0:T(8,128)}), f32[384,384]{1,0:T(8,128)}) %all-reduce.2.cloned.1.call-update) | async-done | bytes 589840 | tf_op jit(solution)/shard_map/psum | solution.py:66
  (48 shorter events, 25.0 us)
Async XLA Ops:
  7.2 1.8 copy-start
  9.5 5.8 copy-start.3
  11.0 22.7 %all-to-all-start = ((bf16[4,512,384]{1,2,0:T(8,128)(2,1)}), bf16[4,512,384]{1,2,0:T(8,128)(2,1)S(1)}, u32[]{:S(2)}, u32[]{:S(2)}) async-start(bf16[4,512,384]{1,2,0:T(8,128)(2,1)} %stack.6), calls=%async_computation | async-start | bytes 3145728 | tf_op jit(solution)/shard_map/all_to_all | solution.py:53
  35.7 19.4 %collective-permute-start = (bf16[2,1536]{0,1:T(8,128)(2,1)S(1)}, bf16[2,1536]{0,1:T(8,128)(2,1)S(1)}, u32[]{:S(2)}, u32[]{:S(2)}) collective-permute-start(bf16[2,1536]{0,1:T(8,128)(2,1)S(1)} %get-tuple-element.9), channel_id=1, source_target_pairs={{0,4},{4,8},{8,12},{12,16},{16,20},{20,24},{24,28},{28,32},{32,36}... | collective-permute-start | bytes 18440 | tf_op jit(solution)/shard_map/ppermute | solution.py:18
  39.5 12.7 %collective-permute-start.1 = (bf16[2,1536]{0,1:T(8,128)(2,1)S(1)}, bf16[2,1536]{0,1:T(8,128)(2,1)S(1)}, u32[]{:S(2)}, u32[]{:S(2)}) collective-permute-start(bf16[2,1536]{0,1:T(8,128)(2,1)S(1)} %get-tuple-element.10), channel_id=1, source_target_pairs={{4,0},{8,4},{12,8},{16,12},{20,16},{24,20},{28,24},{32,28},{36,32}... | collective-permute-start | bytes 18440 | tf_op jit(solution)/shard_map/ppermute | solution.py:19
  59.4 23.3 %all-to-all-start.1 = ((bf16[4,512,384]{1,2,0:T(8,128)(2,1)}), bf16[4,512,384]{1,2,0:T(8,128)(2,1)S(1)}, u32[]{:S(2)}, u32[]{:S(2)}) async-start(bf16[4,512,384]{1,2,0:T(8,128)(2,1)} %stack.7), calls=%async_computation.1 | async-start | bytes 3145728 | tf_op jit(solution)/shard_map/all_to_all | solution.py:53
  84.7 13.0 %collective-permute-start.3 = (bf16[4,1536]{0,1:T(8,128)(2,1)S(1)}, bf16[4,1536]{0,1:T(8,128)(2,1)S(1)}, u32[]{:S(2)}, u32[]{:S(2)}) collective-permute-start(bf16[4,1536]{0,1:T(8,128)(2,1)S(1)} %get-tuple-element.8), channel_id=1, source_target_pairs={{4,0},{8,4},{12,8},{16,12},{20,16},{24,20},{28,24},{32,28},{36,32}... | collective-permute-start | bytes 36872 | tf_op jit(solution)/shard_map/ppermute | solution.py:19
  89.8 12.9 %collective-permute-start.2 = (bf16[4,1536]{0,1:T(8,128)(2,1)S(1)}, bf16[4,1536]{0,1:T(8,128)(2,1)S(1)}, u32[]{:S(2)}, u32[]{:S(2)}) collective-permute-start(bf16[4,1536]{0,1:T(8,128)(2,1)S(1)} %get-tuple-element.7), channel_id=1, source_target_pairs={{0,4},{4,8},{8,12},{12,16},{16,20},{20,24},{24,28},{28,32},{32,36}... | collective-permute-start | bytes 36872 | tf_op jit(solution)/shard_map/ppermute | solution.py:18
  107.0 23.3 %all-to-all-start.2 = ((bf16[4,512,384]{1,2,0:T(8,128)(2,1)}), bf16[4,512,384]{1,2,0:T(8,128)(2,1)S(1)}, u32[]{:S(2)}, u32[]{:S(2)}) async-start(bf16[4,512,384]{1,2,0:T(8,128)(2,1)} %stack.8), calls=%async_computation.2 | async-start | bytes 3145728 | tf_op jit(solution)/shard_map/all_to_all | solution.py:53
  111.9 699.5 %all-reduce.2.cloned.1.call-start = ((), (), s32[]{:S(2)}) async-start(), calls=%async_computation.3 | async-start | bytes 1179648 | tf_op jit(solution)/shard_map/psum | solution.py:66
  132.3 14.2 %collective-permute-start.5 = (bf16[8,1536]{0,1:T(8,128)(2,1)S(1)}, bf16[8,1536]{0,1:T(8,128)(2,1)S(1)}, u32[]{:S(2)}, u32[]{:S(2)}) collective-permute-start(bf16[8,1536]{0,1:T(8,128)(2,1)S(1)} %get-tuple-element.6), channel_id=1, source_target_pairs={{4,0},{8,4},{12,8},{16,12},{20,16},{24,20},{28,24},{32,28},{36,32}... | collective-permute-start | bytes 73736 | tf_op jit(solution)/shard_map/ppermute | solution.py:19
  137.2 14.1 %collective-permute-start.4 = (bf16[8,1536]{0,1:T(8,128)(2,1)S(1)}, bf16[8,1536]{0,1:T(8,128)(2,1)S(1)}, u32[]{:S(2)}, u32[]{:S(2)}) collective-permute-start(bf16[8,1536]{0,1:T(8,128)(2,1)S(1)} %get-tuple-element.5), channel_id=1, source_target_pairs={{0,4},{4,8},{8,12},{12,16},{16,20},{20,24},{24,28},{28,32},{32,36}... | collective-permute-start | bytes 73736 | tf_op jit(solution)/shard_map/ppermute | solution.py:18
  149.4 4.8 copy-start.1
  149.4 6.1 copy-start.2
Sparse Core Ops, SparseCore 0:
  155.5 655.8 all-reduce.1
